TPU v7x, 256 devices: a whole 4x4x8 slice. The times are simulated.
256 devices in a mesh: grp: 4 (over x), box: 64 (over y, z, core).
Axes of the slice: x: 4, y: 4, z: 8, core: 2. Of those that a mesh axis runs over, the one named last changes fastest.
Arguments:
- source: float32 [128, 64, 16, 128], P('grp', 'box'), may hold values from -6 to 6
- alpha_coef: float32 [128, 64, 16, 128], P('grp', 'box'), may hold values from 0.02 to 0.2
- beta_coef: float32 [128, 64, 16, 128], P('grp', 'box'), may hold values from 0.5 to 5
Outputs:
- solution: float32 [128, 64, 16, 128], P('grp', 'box')
All inputs are finite; a program needn't handle non-finite values.
Results may differ from a plain program's by a relative error of at most 0.00002.
Values sent between devices are 32-bit elements; how exact they have to be, the bound alone decides.
A program may use at most 128 MiB of HBM per device.

v0:
```python
import jax
import jax.numpy as jnp
from jax import lax
from jax.experimental import pallas as pl
from jax.experimental.pallas import tpu as pltpu
from jax.sharding import PartitionSpec as P

OMEGA = 0.7
F32 = jnp.float32
MESH = pl.DeviceIdType.MESH
LANES = 128

DIRECTIONS = [(dx, dp) for dx in (-1, 0, 1) for dp in (-2, -1, 0, 1, 2) if (dx, dp) != (0, 0)]
DIAGONALS = [(-1, -1), (-1, 1), (1, -1), (1, 1)]


class Level:
    def __init__(self, own_x, own_y, right, rows, off_y, stretch, scale):
        self.own_x, self.own_y, self.right, self.rows = own_x, own_y, right, rows
        self.off_y, self.stretch, self.scale = off_y, stretch, scale


L0 = Level(32, 16, 4, 40, 3, 1, 1.0)
L1 = Level(16, 8, 8, 32, 6, 2, 0.25)
L2 = Level(8, 4, 8, 24, 8, 4, 0.0625)

SCRATCH = {}
for name in ("nf", "na", "nb"):
    SCRATCH[name] = (640, LANES)
for name in ("ef", "ea", "eb", "w0", "x0", "v0"):
    SCRATCH[name] = (22, 40, LANES)
COEFS = ("cxp", "cxm", "cyp", "cym", "czp", "czm", "inv", "dia", "g")
for name in COEFS:
    SCRATCH[name + "0"] = (22, 40, LANES)
    SCRATCH[name + "1"] = (20, 32, LANES)
    SCRATCH[name + "2"] = (20, 24, LANES)
SCRATCH["syf"] = (2, 2, 32, LANES)
SCRATCH["sya"] = (2, 2, 32, LANES)
SCRATCH["syb"] = (2, 3, 32, LANES)
SCRATCH["sc"] = (4, 16, LANES)
SCRATCH["lc"] = (4, 16, LANES)
SCRATCH["lv"] = (2, 2, 40, LANES)
SCRATCH["rs0"] = (16, 32, LANES)
for name in ("p1f", "p1a", "p1b"):
    SCRATCH[name] = (10, 32, LANES)
for name in ("u1f", "u1a", "u1b", "v1", "w1", "x1"):
    SCRATCH[name] = (20, 32, LANES)
SCRATCH["rs1"] = (8, 16, LANES)
SCRATCH["p2c"] = (2, 5, 24, LANES)
SCRATCH["p2f"] = (5, 24, LANES)
for name in ("u2f", "u2a", "u2b", "w2", "x2"):
    SCRATCH[name] = (20, 24, LANES)
SCRATCH["t1"] = (8, 32, LANES)
SCRATCH["t0"] = (10, 40, LANES)
SCRATCH["out"] = (512, LANES)
N_MESSAGES = 64


def gray(place):
    return place ^ (place >> 1)


def each(low, high, step, work):
    count = (high - low) // step
    if count == 1:
        work(low)
    else:

        @pl.loop(0, count)
        def _(k):
            work(low + k * step)


def lane_index(shape):
    return lax.broadcasted_iota(jnp.int32, shape, len(shape) - 1)


def shift(values, axis, amount):
    size = values.shape[axis]
    return pltpu.roll(values, (-amount) % size, axis)


def pair_lanes(values, width):
    lanes = lane_index(values.shape)
    low_half = (lanes // width) % 2 == 0
    axis = values.ndim - 1
    return values + jnp.where(low_half, shift(values, axis, width), shift(values, axis, -width))


def pack2(even, odd):
    return jnp.where(lane_index(even.shape) % 2 == 0, even, odd)


def pack4(planes):
    lanes = lane_index(planes[0].shape) % 4
    packed = planes[3]
    for k in (2, 1, 0):
        packed = jnp.where(lanes == k, planes[k], packed)
    return packed


def unpack2(packed):
    even = lane_index(packed.shape) % 2 == 0
    axis = packed.ndim - 1
    return jnp.where(even, packed, shift(packed, axis, -1)), jnp.where(even, shift(packed, axis, 1), packed)


def unpack4(packed):
    lanes = lane_index(packed.shape) % 4
    axis = packed.ndim - 1
    moved = {d: (packed if d == 0 else shift(packed, axis, d)) for d in range(-3, 4)}
    planes = []
    for k in range(4):
        plane = moved[k - 3]
        for j in (2, 1, 0):
            plane = jnp.where(lanes == j, moved[k - j], plane)
        planes.append(plane)
    return planes


def make_kernel(groups, boxes):
    names = list(SCRATCH)

    def kernel(f_hbm, a_hbm, b_hbm, o_hbm, *scratch):
        r = dict(zip(names, scratch[: len(names)]))
        load_sem, store_sem, send_sem, recv_sem = scratch[len(names) :]
        gx = lax.axis_index("grp")
        code = lax.axis_index("box")
        pos = code
        for bits in range(1, (boxes - 1).bit_length()):
            pos = pos ^ (code >> bits)

        def exists(dx, dp):
            nx, npos = gx + dx, pos + dp
            return (nx >= 0) & (nx < groups) & (npos >= 0) & (npos < boxes)

        def device(dx, dp):
            nx = lax.rem(gx + dx + groups, groups)
            npos = lax.rem(pos + dp + boxes, boxes)
            return (nx, gray(npos))

        serial = [0]
        sent = []

        def message(direction, source, target):
            k = serial[0]
            serial[0] += 1
            copy = pltpu.make_async_remote_copy(
                src_ref=source,
                dst_ref=target,
                send_sem=send_sem.at[k],
                recv_sem=recv_sem.at[k],
                device_id=device(*direction),
                device_id_type=MESH,
            )
            return direction, copy

        def start(messages):
            for direction in dict.fromkeys(d for d, copy in messages):

                @pl.when(exists(*direction))
                def _():
                    for d, copy in messages:
                        if d == direction:
                            copy.start()

            sent.extend(messages)

        def arrive(messages):
            for direction in dict.fromkeys(d for d, copy in messages):

                @pl.when(exists(-direction[0], -direction[1]))
                def _():
                    for d, copy in messages:
                        if d == direction:
                            copy.wait_recv()

        loads = [
            pltpu.make_async_copy(hbm, r[name].at[pl.ds(0, 512)], load_sem.at[k])
            for k, (hbm, name) in enumerate(((b_hbm, "nb"), (f_hbm, "nf"), (a_hbm, "na")))
        ]
        for copy in loads:
            copy.start()

        def preset(ref, value):
            ref[...] = jnp.full(ref.shape, value, F32)

        for suffix, value in (("f", 0.0), ("a", 1.0), ("b", 0.0)):
            preset(r["n" + suffix].at[pl.ds(512, 128)], value)
            preset(r["e" + suffix].at[pl.ds(0, 3)], value)
            preset(r["e" + suffix].at[pl.ds(19, 3)], value)
            preset(r["p1" + suffix], value)
        corner_row = lax.broadcasted_iota(jnp.int32, (4, 16, LANES), 1)
        r["lc"][...] = jnp.where((corner_row >= 4) & (corner_row < 8), 1.0, 0.0).astype(F32)
        preset(r["lv"], 0.0)
        preset(r["p2f"], 0.0)
        preset(r["p2c"].at[0], 1.0)
        preset(r["p2c"].at[1], 0.0)

        barrier = pltpu.get_barrier_semaphore()
        expected = jnp.int32(0)
        for direction in DIRECTIONS:
            there = exists(*direction)
            expected = expected + there.astype(jnp.int32)

            @pl.when(there)
            def _():
                pl.semaphore_signal(barrier, inc=1, device_id=device(*direction), device_id_type=MESH)

        for copy in loads:
            copy.wait()

        for suffix, width in (("b", 3), ("f", 2), ("a", 2)):
            native, stage = r["n" + suffix], r["sy" + suffix]
            for k in range(width):
                stage[0, k] = native[pl.ds(16 - width + k, 32, stride=16), :]
                stage[1, k] = native[pl.ds(k, 32, stride=16), :]
        for d, (dx, dp) in enumerate(DIAGONALS):
            x = 28 if dx > 0 else 0
            near, far = (15, 14) if dp > 0 else (0, 1)
            for q, (name, y) in enumerate((("nf", near), ("na", near), ("nb", near), ("nb", far))):
                r["sc"][d, 4 * q : 4 * q + 4] = r[name][pl.ds(x * 16 + y, 4, stride=16), :]

        rim = []
        for dp in (-1, 1):
            side = 0 if dp > 0 else 1
            for suffix, width in (("b", 3), ("f", 2), ("a", 2)):
                at = 3 - width if dp > 0 else 19
                rim.append(
                    message(
                        (0, dp),
                        r["sy" + suffix].at[side],
                        r["e" + suffix].at[pl.ds(at, width), pl.ds(0, 32)],
                    )
                )
        for d, direction in enumerate(DIAGONALS):
            rim.append(message(direction, r["sc"].at[d], r["lc"].at[d]))
        rim_x = []
        for dx in (-1, 1):
            for suffix, hbm, width in (("b", b_hbm, 4), ("f", f_hbm, 3), ("a", a_hbm, 3)):
                if dx > 0:
                    source, target = 16 * (32 - width), 16 * (40 - width)
                else:
                    source, target = 0, 512
                rim_x.append(
                    message(
                        (dx, 0),
                        hbm.at[pl.ds(source, 16 * width)],
                        r["n" + suffix].at[pl.ds(target, 16 * width)],
                    )
                )
        pl.semaphore_wait(barrier, expected)
        start(rim)
        start(rim_x)

        for suffix in ("b", "a"):
            native, flat, packed = r["n" + suffix], r["u1" + suffix], r["p1" + suffix]
            for j in range(8):
                total = native[pl.ds(2 * j, 16, stride=32), :] + native[pl.ds(2 * j + 16, 16, stride=32), :]
                total = total + native[pl.ds(2 * j + 1, 16, stride=32), :]
                total = total + native[pl.ds(2 * j + 17, 16, stride=32), :]
                flat[6 + j, 0:16] = pair_lanes(total, 1) * 0.125
            for j in range(4):
                packed[3 + j, 0:16] = pack2(flat[6 + 2 * j, 0:16], flat[7 + 2 * j, 0:16])
            planes = []
            for j in range(4):
                total = flat[6 + 2 * j, pl.ds(0, 8, stride=2), :] + flat[6 + 2 * j, pl.ds(1, 8, stride=2), :]
                total = total + flat[7 + 2 * j, pl.ds(0, 8, stride=2), :]
                total = total + flat[7 + 2 * j, pl.ds(1, 8, stride=2), :]
                planes.append(pair_lanes(total, 2) * 0.125)
            r["p2c"][0 if suffix == "a" else 1, 2, 0:8] = pack4(planes)

        coarse_y = []
        for dp in (-1, 1):
            for name, width in (("p1b", 3), ("p1a", 2)):
                source = 7 - width if dp > 0 else 3
                target = 3 - width if dp > 0 else 7
                coarse_y.append(
                    message(
                        (0, dp),
                        r[name].at[pl.ds(source, width), pl.ds(0, 16)],
                        r[name].at[pl.ds(target, width), pl.ds(0, 16)],
                    )
                )
        for dp in (-2, -1, 1, 2):
            coarse_y.append(
                message(
                    (0, dp),
                    r["p2c"].at[:, 2, pl.ds(0, 8)],
                    r["p2c"].at[:, 2 - dp, pl.ds(0, 8)],
                )
            )
        start(coarse_y)

        def coefficients(level, tag, b, a, low, high, step, f=None):
            c = {name: r[name + tag] for name in COEFS}
            half = 0.5 * level.scale
            shape = (step, level.rows, LANES)
            lanes = lane_index(shape)
            keep_up = lanes < LANES - level.stretch
            keep_down = lanes >= level.stretch
            row = lax.broadcasted_iota(jnp.int32, shape, 1)
            row = jnp.where(row < level.own_x + level.right, row, row - level.rows) + gx * level.own_x
            row_ok = (row >= 0) & (row < groups * level.own_x)
            plane = lax.broadcasted_iota(jnp.int32, shape, 0)

            def work(i):
                here = pl.ds(i, step)
                centre = b[here]
                xp = half * (centre + shift(centre, 1, 1))
                xm = half * (centre + shift(centre, 1, -1))
                yp = half * (centre + b[pl.ds(i + 1, step)])
                ym = half * (centre + b[pl.ds(i - 1, step)])
                zp = half * (centre + jnp.where(keep_up, shift(centre, 2, level.stretch), 0.0))
                zm = half * (centre + jnp.where(keep_down, shift(centre, 2, -level.stretch), 0.0))
                diagonal = a[here] + (((xp + xm) + (yp + ym)) + (zp + zm))
                y = plane + (i - level.off_y + pos * level.own_y)
                ok = row_ok & (y >= 0) & (y < boxes * level.own_y)
                inverse = jnp.where(ok, OMEGA / diagonal, 0.0)
                c["cxp"][here] = xp
                c["cxm"][here] = xm
                c["cyp"][here] = yp
                c["cym"][here] = ym
                c["czp"][here] = jnp.where(keep_up, zp, 0.0)
                c["czm"][here] = jnp.where(keep_down, zm, 0.0)
                c["dia"][here] = diagonal
                c["inv"][here] = inverse
                if f is not None:
                    c["g"][here] = inverse * f[here]

            each(low, high, step, work)

        def spread(level, tag, field, i, step, rows=None):
            c = {name: r[name + tag] for name in COEFS}
            here = pl.ds(i, step)
            centre = field[here]
            up, down = field[pl.ds(i + 1, step)], field[pl.ds(i - 1, step)]
            cut = (lambda v: v) if rows is None else (lambda v: v[:, :rows])
            xs = c["cxp"][here] * shift(centre, 1, 1) + c["cxm"][here] * shift(centre, 1, -1)
            ys = c["cyp"][here] * up + c["cym"][here] * down
            zs = c["czp"][here] * shift(centre, 2, level.stretch) + c["czm"][here] * shift(centre, 2, -level.stretch)
            return cut(centre), cut(xs + ys + zs)

        def second_sweep(level, tag, target, low, high, step):
            def work(i):
                here = pl.ds(i, step)
                centre, total = spread(level, tag, r["g" + tag], i, step)
                target[here] = 1.3 * centre + r["inv" + tag][here] * total

            each(low, high, step, work)

        def sweep(level, tag, field, target, low, high, step):
            def work(i):
                here = pl.ds(i, step)
                centre, total = spread(level, tag, field, i, step)
                target[here] = (0.3 * centre + r["g" + tag][here]) + r["inv" + tag][here] * total

            each(low, high, step, work)

        def residual(level, tag, field, f, target, low, high, step):
            rows = level.own_x

            def work(i):
                here = pl.ds(i, step)
                centre, total = spread(level, tag, field, i, step, rows)
                target[pl.ds(i - level.off_y, step)] = f[here, 0:rows] - r["dia" + tag][here, 0:rows] * centre + total

            each(low, high, step, work)

        def restrict_plane(source, j, rows, width):
            half = rows // 2
            total = source[2 * j, pl.ds(0, half, stride=2), :] + source[2 * j, pl.ds(1, half, stride=2), :]
            total = total + source[2 * j + 1, pl.ds(0, half, stride=2), :]
            total = total + source[2 * j + 1, pl.ds(1, half, stride=2), :]
            return pair_lanes(total, width) * 0.125

        def restrict_pairs(pairs):
            for k in pairs:
                even = restrict_plane(r["rs0"], 2 * k, 32, 1)
                odd = restrict_plane(r["rs0"], 2 * k + 1, 32, 1)
                r["u1f"][6 + 2 * k, 0:16] = even
                r["u1f"][7 + 2 * k, 0:16] = odd
                r["p1f"][3 + k, 0:16] = pack2(even, odd)

        arrive(rim_x)

        def transpose(y):
            for suffix in ("f", "a", "b"):
                r["e" + suffix][y + 3] = r["n" + suffix][pl.ds(y, 40, stride=16), :]

        each(0, 16, 1, transpose)
        coefficients(L0, "0", r["eb"], r["ea"], 4, 18, 2, r["ef"])
        second_sweep(L0, "0", r["v0"], 5, 17, 3)
        residual(L0, "0", r["v0"], r["ef"], r["rs0"], 6, 16, 2)
        restrict_pairs((1, 2))

        arrive(rim)
        for d, (dx, dp) in enumerate(DIAGONALS):
            row = 36 if dx > 0 else 32
            near, far = (2, 1) if dp > 0 else (19, 20)
            for q, (name, y) in enumerate((("ef", near), ("ea", near), ("eb", near), ("eb", far))):
                r[name][y, row : row + 4] = r["lc"][d, 4 * q : 4 * q + 4]
        coefficients(L0, "0", r["eb"], r["ea"], 1, 4, 3, r["ef"])
        coefficients(L0, "0", r["eb"], r["ea"], 18, 21, 3, r["ef"])
        second_sweep(L0, "0", r["v0"], 2, 5, 3)
        second_sweep(L0, "0", r["v0"], 17, 20, 3)
        residual(L0, "0", r["v0"], r["ef"], r["rs0"], 3, 6, 3)
        residual(L0, "0", r["v0"], r["ef"], r["rs0"], 16, 19, 3)
        restrict_pairs((0, 3))

        second = []
        for dx in (-1, 0, 1):
            for dp in (-1, 0, 1):
                if (dx, dp) == (0, 0):
                    continue
                planes = (5, 2, 1) if dp > 0 else ((3, 2, 7) if dp < 0 else (3, 4, 3))
                rows = (8, 8, 24) if dx > 0 else ((0, 8, 16) if dx < 0 else (0, 16, 0))
                second.append(
                    message(
                        (dx, dp),
                        r["p1f"].at[pl.ds(planes[0], planes[1]), pl.ds(rows[0], rows[1])],
                        r["p1f"].at[pl.ds(planes[2], planes[1]), pl.ds(rows[2], rows[1])],
                    )
                )
        start(second)
        fine = [
            message((0, 1), r["v0"].at[pl.ds(17, 2)], r["lv"].at[0]),
            message((0, -1), r["v0"].at[pl.ds(3, 2)], r["lv"].at[1]),
        ]
        start(fine)

        arrive(coarse_y)
        coarse_x = []
        for dx in (-1, 1):
            source, target = (8, 24) if dx > 0 else (0, 16)
            for name, low, count in (("p1b", 0, 10), ("p1a", 1, 8)):
                coarse_x.append(
                    message(
                        (dx, 0),
                        r[name].at[pl.ds(low, count), pl.ds(source, 8)],
                        r[name].at[pl.ds(low, count), pl.ds(target, 8)],
                    )
                )
            coarse_x.append(
                message(
                    (dx, 0),
                    r["p2c"].at[:, :, pl.ds(0, 8)],
                    r["p2c"].at[:, :, pl.ds(16 if dx > 0 else 8, 8)],
                )
            )
        start(coarse_x)
        arrive(coarse_x)

        def unpack_pairs(packed, flat, low, high):
            def work(k):
                even, odd = unpack2(packed[k])
                flat[2 * k] = even
                flat[2 * k + 1] = odd

            each(low, high, 1, work)

        def unpack_quads(packed, flat):
            def work(k):
                for j, plane in enumerate(unpack4(packed[k])):
                    flat[4 * k + j] = plane

            each(0, 5, 1, work)

        unpack_pairs(r["p1b"], r["u1b"], 0, 10)
        unpack_pairs(r["p1a"], r["u1a"], 1, 9)
        coefficients(L1, "1", r["u1b"], r["u1a"], 2, 18, 4)
        unpack_quads(r["p2c"].at[0], r["u2a"])
        unpack_quads(r["p2c"].at[1], r["u2b"])
        coefficients(L2, "2", r["u2b"], r["u2a"], 3, 17, 7)

        arrive(second)
        unpack_pairs(r["p1f"], r["u1f"], 1, 9)

        def first_sweep(tag, f, low, high, step):
            def work(i):
                here = pl.ds(i, step)
                r["g" + tag][here] = r["inv" + tag][here] * f[here]

            each(low, high, step, work)

        first_sweep("1", r["u1f"], 2, 18, 8)
        second_sweep(L1, "1", r["v1"], 3, 17, 7)
        residual(L1, "1", r["v1"], r["u1f"], r["rs1"], 6, 14, 4)
        r["p2f"][2, 0:8] = pack4([restrict_plane(r["rs1"], j, 16, 2) for j in range(4)])

        third = []
        for dx, dp in DIRECTIONS:
            row = 16 if dx > 0 else (8 if dx < 0 else 0)
            third.append(
                message((dx, dp), r["p2f"].at[2, pl.ds(0, 8)], r["p2f"].at[2 - dp, pl.ds(row, 8)])
            )
        start(third)
        arrive(third)

        unpack_quads(r["p2f"], r["u2f"])
        first_sweep("2", r["u2f"], 3, 17, 7)
        second_sweep(L2, "2", r["w2"], 4, 16, 6)
        sweep(L2, "2", r["w2"], r["x2"], 5, 15, 5)
        sweep(L2, "2", r["x2"], r["w2"], 6, 14, 4)

        for q in range(6, 14):
            for half in (0, 1):
                r["t1"][q - 6, pl.ds(half, 12, stride=2), :] = r["w2"][q, 0:12]
                r["t1"][q - 6, pl.ds(24 + half, 4, stride=2), :] = r["w2"][q, 20:24]
            for half in (0, 1):
                i = 2 * q - 10 + half
                r["w1"][i] = r["v1"][i] + r["t1"][q - 6]
        sweep(L1, "1", r["w1"], r["x1"], 4, 16, 6)
        sweep(L1, "1", r["x1"], r["w1"], 5, 15, 5)

        arrive(fine)
        for q in range(5, 15):
            for half in (0, 1):
                r["t0"][q - 5, pl.ds(half, 18, stride=2), :] = r["w1"][q, 0:18]
                r["t0"][q - 5, pl.ds(36 + half, 2, stride=2), :] = r["w1"][q, 30:32]
            for half in (0, 1):
                i = 2 * q - 9 + half
                if q == 5:
                    before = r["lv"][0, half]
                elif q == 14:
                    before = r["lv"][1, half]
                else:
                    before = r["v0"][i]
                r["w0"][i] = before + r["t0"][q - 5]
        sweep(L0, "0", r["w0"], r["x0"], 2, 20, 3)

        def last(i):
            centre, total = spread(L0, "0", r["x0"], i, 2)
            here = pl.ds(i, 2)
            value = (0.3 * centre + r["g0"][here]) + r["inv0"][here] * total
            for k in range(2):
                r["out"][pl.ds(i - 3 + k, 32, stride=16), :] = value[k, 0:32]

        each(3, 19, 2, last)
        store = pltpu.make_async_copy(r["out"], o_hbm, store_sem)
        store.start()
        for direction in dict.fromkeys(d for d, copy in sent):

            @pl.when(exists(*direction))
            def _():
                for d, copy in sent:
                    if d == direction:
                        copy.wait_send()

        store.wait()
        assert serial[0] <= N_MESSAGES

    return kernel


def solution(mesh):
    groups, boxes = mesh.shape["grp"], mesh.shape["box"]

    def body(source, alpha_coef, beta_coef):
        flat = [v.reshape(512, LANES) for v in (source, alpha_coef, beta_coef)]
        hbm = pl.BlockSpec(memory_space=pl.ANY)
        out = pl.pallas_call(
            make_kernel(groups, boxes),
            out_shape=jax.ShapeDtypeStruct((512, LANES), F32),
            in_specs=[hbm, hbm, hbm],
            out_specs=hbm,
            scratch_shapes=[pltpu.VMEM(shape, F32) for shape in SCRATCH.values()]
            + [
                pltpu.SemaphoreType.DMA((3,)),
                pltpu.SemaphoreType.DMA,
                pltpu.SemaphoreType.DMA((N_MESSAGES,)),
                pltpu.SemaphoreType.DMA((N_MESSAGES,)),
            ],
            compiler_params=pltpu.CompilerParams(
                collective_id=0, has_side_effects=True, vmem_limit_bytes=48 * 1024 * 1024
            ),
        )(*flat)
        return out.reshape(32, 1, 16, LANES)

    spec = P("grp", "box", None, None)
    return jax.shard_map(body, mesh=mesh, in_specs=(spec, spec, spec), out_specs=spec, check_vma=False)
```

profile of v0, /device:TPU:73, one launch (start us, length us, event | category | flops | bytes accessed | tf_op | source)
XLA Modules:
  0.0 37.6 jit_solution(843689339254096290)
XLA Ops:
  0.0 0.0 copy-start
  0.0 0.9 %copy-done = f32[32,1,16,128]{3,2,1,0:T(8,128)S(1)} copy-done((f32[32,1,16,128]{3,2,1,0:T(8,128)S(1)}, f32[32,1,16,128]{3,2,1,0:T(8,128)}, u32[]{:S(2)}) %copy-start) | copy-done | bytes 262168
  1.0 0.0 copy-start.1
  1.0 0.9 %copy-done.1 = f32[32,1,16,128]{3,2,1,0:T(8,128)S(1)} copy-done((f32[32,1,16,128]{3,2,1,0:T(8,128)S(1)}, f32[32,1,16,128]{3,2,1,0:T(8,128)}, u32[]{:S(2)}) %copy-start.1) | copy-done | bytes 262168
  1.9 0.0 copy-start.2
  1.9 0.9 %copy-done.2 = f32[32,1,16,128]{3,2,1,0:T(8,128)S(1)} copy-done((f32[32,1,16,128]{3,2,1,0:T(8,128)S(1)}, f32[32,1,16,128]{3,2,1,0:T(8,128)}, u32[]{:S(2)}) %copy-start.2) | copy-done | bytes 262168
  2.9 34.0 %shard_map.37 = f32[512,128]{1,0:T(8,128)S(1)} custom-call(f32[512,128]{1,0:T(8,128)S(1)} %bitcast.7, f32[512,128]{1,0:T(8,128)S(1)} %bitcast.8, f32[512,128]{1,0:T(8,128)S(1)} %bitcast.9), custom_call_target="tpu_custom_call" | custom-call | tf_op jit(solution)/shard_map/pallas_call | solution.py:562
  36.9 0.7 %copy.6 = f32[32,1,16,128]{3,2,1,0:T(8,128)} copy(f32[32,1,16,128]{3,2,1,0:T(8,128)S(1)} %bitcast.6) | data formatting | bytes 524288
Async XLA Ops:
  0.0 0.9 %copy-start = (f32[32,1,16,128]{3,2,1,0:T(8,128)S(1)}, f32[32,1,16,128]{3,2,1,0:T(8,128)}, u32[]{:S(2)}) copy-start(f32[32,1,16,128]{3,2,1,0:T(8,128)} %param.3) | copy-start | bytes 786436
  1.0 0.9 %copy-start.1 = (f32[32,1,16,128]{3,2,1,0:T(8,128)S(1)}, f32[32,1,16,128]{3,2,1,0:T(8,128)}, u32[]{:S(2)}) copy-start(f32[32,1,16,128]{3,2,1,0:T(8,128)} %param.4) | copy-start | bytes 786436
  1.9 0.9 %copy-start.2 = (f32[32,1,16,128]{3,2,1,0:T(8,128)S(1)}, f32[32,1,16,128]{3,2,1,0:T(8,128)}, u32[]{:S(2)}) copy-start(f32[32,1,16,128]{3,2,1,0:T(8,128)} %param.5) | copy-start | bytes 786436
where the time goes:
time: 37.7 us; the launch traced here: 37.6 us
  Pallas kernels  34 us (90%)
  local copies, waits for them, and re-layouts  3.55 us (9%)
    pallas_call x1, Pallas kernels, body(): pl.pallas_call(make_kernel(groups, boxes), out_shape=jax.ShapeDtypeStruct...  34 us
    unnamed x7, local copies, waits for them, and re-layouts  3.55 us

commit v1 on v0

--- a/solution.py
+++ b/solution.py
@@ -11,6 +11,7 @@
 LANES = 128
 
 DIRECTIONS = [(dx, dp) for dx in (-1, 0, 1) for dp in (-2, -1, 0, 1, 2) if (dx, dp) != (0, 0)]
+DIRECT = [(0, 1), (0, -1), (1, 0), (-1, 0)]
 DIAGONALS = [(-1, -1), (-1, 1), (1, -1), (1, 1)]
 
 
@@ -52,7 +53,6 @@
     SCRATCH[name] = (20, 24, LANES)
 SCRATCH["t1"] = (8, 32, LANES)
 SCRATCH["t0"] = (10, 40, LANES)
-SCRATCH["out"] = (512, LANES)
 N_MESSAGES = 64
 
 
@@ -121,9 +121,9 @@
 def make_kernel(groups, boxes):
     names = list(SCRATCH)
 
-    def kernel(f_hbm, a_hbm, b_hbm, o_hbm, *scratch):
+    def kernel(f_hbm, a_hbm, b_hbm, o_ref, *scratch):
         r = dict(zip(names, scratch[: len(names)]))
-        load_sem, store_sem, send_sem, recv_sem = scratch[len(names) :]
+        load_sem, ready_sem, send_sem, recv_sem = scratch[len(names) :]
         gx = lax.axis_index("grp")
         code = lax.axis_index("box")
         pos = code
@@ -199,7 +199,7 @@
 
         barrier = pltpu.get_barrier_semaphore()
         expected = jnp.int32(0)
-        for direction in DIRECTIONS:
+        for direction in DIRECT:
             there = exists(*direction)
             expected = expected + there.astype(jnp.int32)
 
@@ -233,8 +233,7 @@
                         r["e" + suffix].at[pl.ds(at, width), pl.ds(0, 32)],
                     )
                 )
-        for d, direction in enumerate(DIAGONALS):
-            rim.append(message(direction, r["sc"].at[d], r["lc"].at[d]))
+        corners = [message(direction, r["sc"].at[d], r["lc"].at[d]) for d, direction in enumerate(DIAGONALS)]
         rim_x = []
         for dx in (-1, 1):
             for suffix, hbm, width in (("b", b_hbm, 4), ("f", f_hbm, 3), ("a", a_hbm, 3)):
@@ -251,7 +250,15 @@
                 )
         pl.semaphore_wait(barrier, expected)
         start(rim)
+        for dx in (-1, 1):
+
+            @pl.when(exists(dx, 0))
+            def _():
+                pl.semaphore_signal(ready_sem, inc=1, device_id=device(dx, 0), device_id_type=MESH)
+
         start(rim_x)
+        pl.semaphore_wait(ready_sem, exists(-1, 0).astype(jnp.int32) + exists(1, 0).astype(jnp.int32))
+        start(corners)
 
         for suffix in ("b", "a"):
             native, flat, packed = r["n" + suffix], r["u1" + suffix], r["p1" + suffix]
@@ -282,14 +289,10 @@
                         r[name].at[pl.ds(target, width), pl.ds(0, 16)],
                     )
                 )
-        for dp in (-2, -1, 1, 2):
-            coarse_y.append(
-                message(
-                    (0, dp),
-                    r["p2c"].at[:, 2, pl.ds(0, 8)],
-                    r["p2c"].at[:, 2 - dp, pl.ds(0, 8)],
-                )
-            )
+        coarsest_y = [
+            message((0, dp), r["p2c"].at[:, 2, pl.ds(0, 8)], r["p2c"].at[:, 2 - dp, pl.ds(0, 8)])
+            for dp in (-2, -1, 1, 2)
+        ]
         start(coarse_y)
 
         def coefficients(level, tag, b, a, low, high, step, f=None):
@@ -388,13 +391,15 @@
             for suffix in ("f", "a", "b"):
                 r["e" + suffix][y + 3] = r["n" + suffix][pl.ds(y, 40, stride=16), :]
 
-        each(0, 16, 1, transpose)
+        each(0, 16, 4, lambda y: [transpose(y + n) for n in range(4)])
         coefficients(L0, "0", r["eb"], r["ea"], 4, 18, 2, r["ef"])
         second_sweep(L0, "0", r["v0"], 5, 17, 3)
         residual(L0, "0", r["v0"], r["ef"], r["rs0"], 6, 16, 2)
         restrict_pairs((1, 2))
 
         arrive(rim)
+        arrive(corners)
+        start(coarsest_y)
         for d, (dx, dp) in enumerate(DIAGONALS):
             row = 36 if dx > 0 else 32
             near, far = (2, 1) if dp > 0 else (19, 20)
@@ -441,13 +446,14 @@
                         r[name].at[pl.ds(low, count), pl.ds(target, 8)],
                     )
                 )
-            coarse_x.append(
-                message(
-                    (dx, 0),
-                    r["p2c"].at[:, :, pl.ds(0, 8)],
-                    r["p2c"].at[:, :, pl.ds(16 if dx > 0 else 8, 8)],
-                )
+        coarsest_x = [
+            message(
+                (dx, 0),
+                r["p2c"].at[:, :, pl.ds(0, 8)],
+                r["p2c"].at[:, :, pl.ds(16 if dx > 0 else 8, 8)],
             )
+            for dx in (-1, 1)
+        ]
         start(coarse_x)
         arrive(coarse_x)
 
@@ -457,21 +463,18 @@
                 flat[2 * k] = even
                 flat[2 * k + 1] = odd
 
-            each(low, high, 1, work)
+            each(low, high, 2 if high - low == 10 else 4, lambda k: [work(k + n) for n in range(2 if high - low == 10 else 4)])
 
         def unpack_quads(packed, flat):
             def work(k):
                 for j, plane in enumerate(unpack4(packed[k])):
                     flat[4 * k + j] = plane
 
-            each(0, 5, 1, work)
+            each(0, 5, 5, lambda k: [work(k + n) for n in range(5)])
 
         unpack_pairs(r["p1b"], r["u1b"], 0, 10)
         unpack_pairs(r["p1a"], r["u1a"], 1, 9)
         coefficients(L1, "1", r["u1b"], r["u1a"], 2, 18, 4)
-        unpack_quads(r["p2c"].at[0], r["u2a"])
-        unpack_quads(r["p2c"].at[1], r["u2b"])
-        coefficients(L2, "2", r["u2b"], r["u2a"], 3, 17, 7)
 
         arrive(second)
         unpack_pairs(r["p1f"], r["u1f"], 1, 9)
@@ -483,9 +486,9 @@
 
             each(low, high, step, work)
 
-        first_sweep("1", r["u1f"], 2, 18, 8)
-        second_sweep(L1, "1", r["v1"], 3, 17, 7)
-        residual(L1, "1", r["v1"], r["u1f"], r["rs1"], 6, 14, 4)
+        first_sweep("1", r["u1f"], 2, 18, 16)
+        second_sweep(L1, "1", r["v1"], 3, 17, 14)
+        residual(L1, "1", r["v1"], r["u1f"], r["rs1"], 6, 14, 8)
         r["p2f"][2, 0:8] = pack4([restrict_plane(r["rs1"], j, 16, 2) for j in range(4)])
 
         third = []
@@ -495,13 +498,19 @@
                 message((dx, dp), r["p2f"].at[2, pl.ds(0, 8)], r["p2f"].at[2 - dp, pl.ds(row, 8)])
             )
         start(third)
+        arrive(coarsest_y)
+        start(coarsest_x)
+        arrive(coarsest_x)
+        unpack_quads(r["p2c"].at[0], r["u2a"])
+        unpack_quads(r["p2c"].at[1], r["u2b"])
+        coefficients(L2, "2", r["u2b"], r["u2a"], 3, 17, 7)
         arrive(third)
 
         unpack_quads(r["p2f"], r["u2f"])
-        first_sweep("2", r["u2f"], 3, 17, 7)
-        second_sweep(L2, "2", r["w2"], 4, 16, 6)
-        sweep(L2, "2", r["w2"], r["x2"], 5, 15, 5)
-        sweep(L2, "2", r["x2"], r["w2"], 6, 14, 4)
+        first_sweep("2", r["u2f"], 3, 17, 14)
+        second_sweep(L2, "2", r["w2"], 4, 16, 12)
+        sweep(L2, "2", r["w2"], r["x2"], 5, 15, 10)
+        sweep(L2, "2", r["x2"], r["w2"], 6, 14, 8)
 
         for q in range(6, 14):
             for half in (0, 1):
@@ -510,8 +519,8 @@
             for half in (0, 1):
                 i = 2 * q - 10 + half
                 r["w1"][i] = r["v1"][i] + r["t1"][q - 6]
-        sweep(L1, "1", r["w1"], r["x1"], 4, 16, 6)
-        sweep(L1, "1", r["x1"], r["w1"], 5, 15, 5)
+        sweep(L1, "1", r["w1"], r["x1"], 4, 16, 12)
+        sweep(L1, "1", r["x1"], r["w1"], 5, 15, 10)
 
         arrive(fine)
         for q in range(5, 15):
@@ -527,18 +536,16 @@
                 else:
                     before = r["v0"][i]
                 r["w0"][i] = before + r["t0"][q - 5]
-        sweep(L0, "0", r["w0"], r["x0"], 2, 20, 3)
+        sweep(L0, "0", r["w0"], r["x0"], 2, 20, 9)
 
         def last(i):
-            centre, total = spread(L0, "0", r["x0"], i, 2)
-            here = pl.ds(i, 2)
+            centre, total = spread(L0, "0", r["x0"], i, 8)
+            here = pl.ds(i, 8)
             value = (0.3 * centre + r["g0"][here]) + r["inv0"][here] * total
-            for k in range(2):
-                r["out"][pl.ds(i - 3 + k, 32, stride=16), :] = value[k, 0:32]
-
-        each(3, 19, 2, last)
-        store = pltpu.make_async_copy(r["out"], o_hbm, store_sem)
-        store.start()
+            for k in range(8):
+                o_ref[pl.ds(i - 3 + k, 32, stride=16), :] = value[k, 0:32]
+
+        each(3, 19, 8, last)
         for direction in dict.fromkeys(d for d, copy in sent):
 
             @pl.when(exists(*direction))
@@ -547,7 +554,6 @@
                     if d == direction:
                         copy.wait_send()
 
-        store.wait()
         assert serial[0] <= N_MESSAGES
 
     return kernel
@@ -557,17 +563,17 @@
     groups, boxes = mesh.shape["grp"], mesh.shape["box"]
 
     def body(source, alpha_coef, beta_coef):
-        flat = [v.reshape(512, LANES) for v in (source, alpha_coef, beta_coef)]
-        hbm = pl.BlockSpec(memory_space=pl.ANY)
+        flat = [pltpu.with_memory_space_constraint(v.reshape(512, LANES), pltpu.HBM) for v in (source, alpha_coef, beta_coef)]
+        hbm = pl.BlockSpec(memory_space=pltpu.HBM)
         out = pl.pallas_call(
             make_kernel(groups, boxes),
             out_shape=jax.ShapeDtypeStruct((512, LANES), F32),
             in_specs=[hbm, hbm, hbm],
-            out_specs=hbm,
+            out_specs=pl.BlockSpec(memory_space=pltpu.VMEM),
             scratch_shapes=[pltpu.VMEM(shape, F32) for shape in SCRATCH.values()]
             + [
                 pltpu.SemaphoreType.DMA((3,)),
-                pltpu.SemaphoreType.DMA,
+                pltpu.SemaphoreType.REGULAR,
                 pltpu.SemaphoreType.DMA((N_MESSAGES,)),
                 pltpu.SemaphoreType.DMA((N_MESSAGES,)),
             ],

time: 37.7 us -> 29 us (0.77)
  Pallas kernels: 34 us -> 28.2 us
  local copies, waits for them, and re-layouts: 3.55 us -> 0.71 us
    pallas_call x1, Pallas kernels: 34 us -> 28.2 us  [body(): pl.pallas_call(make_kernel(groups, boxes), out_shape=jax.ShapeDtypeStruct...]
    unnamed x7 -> x1, local copies, waits for them, and re-layouts: 3.55 us -> 0.71 us
where the time goes in v1:
time: 29 us; the launch traced here: 28.9 us
  Pallas kernels  28.2 us (97%)
  local copies, waits for them, and re-layouts  0.71 us (2%)
    pallas_call x1, Pallas kernels, body(): pl.pallas_call(make_kernel(groups, boxes), out_shape=jax.ShapeDtypeStruct...  28.2 us
    unnamed x1, local copies, waits for them, and re-layouts  0.71 us

profile of v1, /device:TPU:73, one launch (start us, length us, event | category | flops | bytes accessed | tf_op | source)
XLA Modules:
  0.0 28.9 jit_solution(2979240149877920283)
XLA Ops:
  0.0 28.2 %shard_map.37 = f32[512,128]{1,0:T(8,128)S(1)} custom-call(f32[512,128]{1,0:T(8,128)} %bitcast.7, f32[512,128]{1,0:T(8,128)} %bitcast.8, f32[512,128]{1,0:T(8,128)} %bitcast.9), custom_call_target="tpu_custom_call" | custom-call | tf_op jit(solution)/shard_map/pallas_call | solution.py:568
  28.2 0.7 %copy.6 = f32[32,1,16,128]{3,2,1,0:T(8,128)} copy(f32[32,1,16,128]{3,2,1,0:T(8,128)S(1)} %bitcast.6) | data formatting | bytes 524288
